TPU v7x, 32 devices: a whole 2x2x4 slice. The times are simulated.
32 devices in a mesh: groups: 2 (over y), tiles: 4 (over z), freq: 2 (over x), field: 2 (over core).
Axes of the slice: x: 2, y: 2, z: 4, core: 2. Of those that a mesh axis runs over, the one named last changes fastest.
Arguments:
- fields: bfloat16 [2, 4, 512, 1024], P('field', 'tiles', ('groups', 'freq')), parts along dimension 2, may hold values from -7.5 to 7.5
- slot_tile_ids: int32 [4], replicated, may hold values from 0 to 3, each once
- neighbour_tile_ids: int32 [4, 4], replicated, may hold values from 0 to 3
- neighbour_rotation_code: int32 [4, 4], replicated, may hold values from 0 to 7
- paired_tile_ids: int32 [4, 2], P('tiles'), may hold values from 0 to 3
Outputs:
- csd: float32 [8, 2, 2, 32, 128, 128], P(('groups', 'tiles'), None, None, ('freq', 'field')), parts along dimension 0
There are 2 independent parts, one for each index of `groups`. A program takes and returns all parts, laid end to end along the dimension named above; an argument that names none is the same for every part. Nothing has to cross between parts.
All inputs are finite; a program needn't handle non-finite values.
Results may differ from a plain program's by a relative error of at most 0.0095.
Values may be sent and summed in bfloat16 or wider, within the bound.
A program may use at most 64 MiB of HBM per device.

v0:
```python
import math
import jax
import jax.numpy as jnp
from jax import lax
from jax.sharding import PartitionSpec as P

SIDE = 32
SEGLEN = 64
diffusion = 0.25


def slot_lookup(slot_tile_ids, tile_ids):
    matches = (slot_tile_ids[None, :] == tile_ids.reshape(-1)[:, None]).astype(jnp.int32)
    positions = jnp.sum(
        matches * jnp.arange(slot_tile_ids.shape[0], dtype=jnp.int32)[None, :], axis=1
    )
    return positions.reshape(tile_ids.shape)


def tile_edges(field, tile_side):
    cell_count = field.shape[-1]
    north = field[..., :tile_side]
    east = field[..., tile_side - 1 :: tile_side]
    south = field[..., cell_count - tile_side :]
    west = field[..., ::tile_side]
    return jnp.stack([north, east, south, west], axis=-3)


def inner_edges(field, tile_side):
    cell_count = field.shape[-1]
    north = field[..., tile_side : 2 * tile_side]
    east = field[..., tile_side - 2 :: tile_side]
    south = field[..., cell_count - 2 * tile_side : cell_count - tile_side]
    west = field[..., 1::tile_side]
    return jnp.stack([north, east, south, west], axis=-3)


def pick_rims(all_edges, near_slots, codes):
    chosen = all_edges[near_slots, codes % 4]
    flipped = chosen[..., ::-1]
    return jnp.where((codes // 4 == 1)[:, :, None, None], flipped, chosen)


def smooth_step(field, rims, tile_side):
    cell_count = field.shape[-1]
    values = field.astype(jnp.float32)
    edge_vals = rims.astype(jnp.float32)
    above_row = jnp.concatenate([edge_vals[:, 0], values[..., : cell_count - tile_side]], axis=-1)
    below_row = jnp.concatenate([values[..., tile_side:], edge_vals[:, 2]], axis=-1)
    column_pos = jnp.arange(cell_count, dtype=jnp.int32) % tile_side
    west_full = jnp.repeat(edge_vals[:, 3], tile_side, axis=-1)
    east_full = jnp.repeat(edge_vals[:, 1], tile_side, axis=-1)
    leftward = jnp.where(column_pos == 0, west_full, jnp.roll(values, 1, axis=-1))
    rightward = jnp.where(column_pos == tile_side - 1, east_full, jnp.roll(values, -1, axis=-1))
    laplace = above_row + below_row + leftward + rightward - 4.0 * values
    return (values + diffusion * laplace).astype(jnp.bfloat16)


def before_along(values, first):
    return jnp.concatenate([first[..., None], values[..., :-1]], axis=-1)


def after_along(values, last):
    return jnp.concatenate([values[..., 1:], last[..., None]], axis=-1)


def smooth_one(values, above, below, leftward, rightward):
    laplace = above + below + leftward + rightward - 4.0 * values
    return (values + diffusion * laplace).astype(jnp.bfloat16)


def edge_sweep(outer, inner, rims):
    outer_vals = outer.astype(jnp.float32)
    inner_vals = inner.astype(jnp.float32)
    rim_vals = rims.astype(jnp.float32)
    north_rim = rim_vals[:, 0]
    east_rim = rim_vals[:, 1]
    south_rim = rim_vals[:, 2]
    west_rim = rim_vals[:, 3]
    north = outer_vals[:, 0]
    east = outer_vals[:, 1]
    south = outer_vals[:, 2]
    west = outer_vals[:, 3]
    new_north = smooth_one(
        north,
        north_rim,
        inner_vals[:, 0],
        before_along(north, west_rim[..., 0]),
        after_along(north, east_rim[..., 0]),
    )
    new_east = smooth_one(
        east,
        before_along(east, north_rim[..., -1]),
        after_along(east, south_rim[..., -1]),
        inner_vals[:, 1],
        east_rim,
    )
    new_south = smooth_one(
        south,
        inner_vals[:, 2],
        south_rim,
        before_along(south, west_rim[..., -1]),
        after_along(south, east_rim[..., -1]),
    )
    new_west = smooth_one(
        west,
        before_along(west, north_rim[..., 0]),
        after_along(west, south_rim[..., 0]),
        west_rim,
        inner_vals[:, 3],
    )
    return jnp.stack([new_north, new_east, new_south, new_west], axis=1)


def coarse_sums(field, tile_side):
    leading = field.shape[:-1]
    blocks = field.astype(jnp.float32).reshape(leading + (tile_side // 2, 2, tile_side // 4, 4))
    return jnp.sum(blocks, axis=(-3, -1)).reshape(leading + (tile_side // 2 * (tile_side // 4),))


def window_table(seg_length):
    samples = jnp.arange(seg_length, dtype=jnp.int32)
    frequency = jnp.arange(seg_length // 2, dtype=jnp.int32)
    products = frequency[:, None] * samples[None, :] % seg_length
    angles = 2.0 * math.pi / seg_length * products.astype(jnp.float32)
    window = 0.5 - 0.5 * jnp.cos(2.0 * math.pi / seg_length * samples.astype(jnp.float32))
    dft_table = jnp.stack([window[None, :] * jnp.cos(angles), -window[None, :] * jnp.sin(angles)])
    return (dft_table, jnp.sum(window * window))


def segment_spectra(coarse, dft_table):
    leading = coarse.shape[0]
    segments = coarse.reshape(leading, -1, dft_table.shape[-1], coarse.shape[-1])
    spectra = jnp.einsum("cft,nstp->nscfp", dft_table, segments, precision=lax.Precision.HIGHEST)
    return spectra.astype(jnp.bfloat16)


def cross_density(height, partner, window_power):
    rotated = jnp.stack([height[:, :, 1], -height[:, :, 0]], axis=2)
    stacked = jnp.stack([height, rotated], axis=1)
    cross = jnp.einsum(
        "noscfi,nkscfj->nkofij", stacked, partner, preferred_element_type=jnp.float32
    )
    return cross / (partner.shape[2] * window_power)


def shards(fields, slot_tile_ids, neighbour_tile_ids, neighbour_rotation_code, paired_tile_ids):
    field = fields[0]
    local_count = field.shape[0]
    first_local = lax.axis_index("tiles") * local_count
    near_all = slot_lookup(slot_tile_ids, neighbour_tile_ids)
    near_local = lax.dynamic_slice_in_dim(near_all, first_local, local_count, 0)
    code_local = lax.dynamic_slice_in_dim(neighbour_rotation_code, first_local, local_count, 0)
    every_outer = lax.all_gather(tile_edges(field, SIDE), "tiles", axis=0, tiled=True)
    every_inner = lax.all_gather(inner_edges(field, SIDE), "tiles", axis=0, tiled=True)
    every_rim = pick_rims(every_outer, near_all, neighbour_rotation_code)
    local_rim = lax.dynamic_slice_in_dim(every_rim, first_local, local_count, 0)
    field = smooth_step(field, local_rim, SIDE)
    new_edges = edge_sweep(every_outer, every_inner, every_rim)
    field = smooth_step(field, pick_rims(new_edges, near_local, code_local), SIDE)
    dft_table, window_power = window_table(SEGLEN)
    spectra = segment_spectra(coarse_sums(field, SIDE), dft_table)
    banded = lax.all_to_all(
        lax.all_to_all(spectra[None], "freq", split_axis=4, concat_axis=2, tiled=True),
        "field",
        split_axis=4,
        concat_axis=0,
        tiled=True,
    )
    partner_slots = slot_lookup(slot_tile_ids, paired_tile_ids)
    every_band = lax.all_gather(banded, "tiles", axis=1, tiled=True)
    first_slot = lax.axis_index("tiles") * banded.shape[1]
    height = lax.dynamic_slice_in_dim(every_band[0], first_slot, banded.shape[1], 0)
    velocity = every_band[1]
    return cross_density(height, velocity[partner_slots], window_power)


def solution(mesh):
    placed = (P("field", "tiles", ("groups", "freq"), None), P(), P(), P(), P("tiles", None))
    return jax.shard_map(
        shards,
        mesh=mesh,
        in_specs=placed,
        out_specs=P(("groups", "tiles"), None, None, ("freq", "field"), None, None),
        check_vma=False,
    )
```

profile of v0, /device:TPU:0, one launch (start us, length us, event | category | flops | bytes accessed | tf_op | source)
XLA Modules:
  0.0 69.6 jit_solution(6394495090829797569)
XLA Ops:
  0.1 0.8 %eq.65 = s32[16]{0:T(128)S(1)} reshape(s32[4,4]{1,0:T(4,128)} %param.7) | data formatting | bytes 128 | tf_op jit(solution)/shard_map/eq | solution.py:13
  0.9 0.7 %select_reduce_fusion = s32[16]{0:T(128)S(1)} fusion(s32[16]{0:T(128)S(1)} %eq.65, s32[4]{0:T(128)} %param.6), kind=kLoop, calls=%fused_computation.163 | loop fusion | flops 176 | bytes 144 | tf_op jit(solution)/shard_map/reduce_sum | solution.py:14
  1.6 0.1 reshape.896
  1.7 0.1 reshape.895
  1.8 0.1 broadcast_compare_fusion
  1.9 1.1 %copy.181 = bf16[1,1,128,1024]{2,3,1,0:T(8,128)(2,1)S(1)} copy(bf16[1,1,128,1024]{3,2,1,0:T(8,128)(2,1)} %param.5) | data formatting | bytes 524288 | tf_op args[0]
  3.0 0.1 slice.203
  3.0 0.1 slice.187
  3.1 0.1 slice.201
  3.2 0.1 slice.185
  3.3 0.0 copy-start
  3.3 1.0 %fusion.83 = (f32[1,128,992]{1,2,0:T(8,128)}, f32[1,128,992]{1,2,0:T(8,128)}) fusion(f32[1,128,1024]{1,2,0:T(8,128)S(1)} %bitcast_convert_fusion), kind=kLoop, calls=%fused_computation.197 | loop fusion | bytes 2031616 | tf_op jit(solution)/shard_map/slice | solution.py:48
  4.3 0.1 fusion.81
  4.4 0.0 copy-done
  4.5 0.1 reshape.901
  4.6 15.1 %all_gather.9 = bf16[4,4,128,32]{2,3,1,0:T(8,128)(2,1)S(1)} all-gather(bf16[1,4,128,32]{2,3,1,0:T(8,128)(2,1)S(1)} %pad_maximum_fusion.5), channel_id=1, replica_groups=mesh['groups'=2,'tiles'=4,'freq'=2,'field'=2] {'tiles'}, dimensions={0}, use_global_device_ids=true | all-gather | bytes 163840 | tf_op jit(solution)/shard_map/all_gather | solution.py:154
  19.7 0.6 gather_fusion
  20.3 0.1 rev.6
  20.3 0.1 fusion.77
  20.5 2.2 %fusion.14 = (f32[1,128,1024]{1,2,0:T(8,128)S(1)}, f32[1,128,1024]{1,2,0:T(8,128)S(1)}, f32[1,128,1024]{1,2,0:T(8,128)S(1)}, f32[1,128,1024]{1,2,0:T(8,128)S(1)}) fusion(f32[128,32]{0,1:T(8,128)S(1)} %get-tuple-element.45, f32[128,32]{0,1:T(8,128)S(1)} %get-tuple-element.44, pred[1024]{0:T(1024)(128)(4,1)S(1)} %get-tuple-element.75, ...), kind=kLoop, calls=%fused_computation.32 | loop fusion | flops 2097152 | bytes 4491264 | tf_op jit(solution)/shard_map/convert_element_type | solution.py:46
  22.7 1.0 %fusion.80 = (f32[1,128,992]{1,2,0:T(8,128)}, f32[1,128,992]{1,2,0:T(8,128)}) fusion(f32[1,128,1024]{1,2,0:T(8,128)S(1)} %get-tuple-element.9), kind=kLoop, calls=%fused_computation.194 | loop fusion | bytes 2031616 | tf_op jit(solution)/shard_map/slice | solution.py:49
  23.7 0.1 fusion.79
  23.8 13.5 %all_gather.10 = bf16[4,4,128,32]{2,3,1,0:T(8,128)(2,1)S(1)} all-gather(bf16[1,4,128,32]{2,3,1,0:T(8,128)(2,1)S(1)} %pad_maximum_fusion.6), channel_id=1, replica_groups=mesh['groups'=2,'tiles'=4,'freq'=2,'field'=2] {'tiles'}, dimensions={0}, use_global_device_ids=true | all-gather | bytes 163840 | tf_op jit(solution)/shard_map/all_gather | solution.py:155
  37.5 0.1 fusion.41
  37.6 0.1 fusion.33
  37.7 0.6 gather_fusion.1
  38.3 0.1 fusion.50
  38.5 1.2 %maximum_add_fusion.1 = f32[1,128,1024]{1,2,0:T(8,128)S(1)} fusion(f32[1,128,992]{1,2,0:T(8,128)} %get-tuple-element.22, f32[1,128,32]{1,2,0:T(8,128)S(1)} %get-tuple-element.52, f32[1,128,32]{1,2,0:T(8,128)S(1)} %get-tuple-element.51, f32[1,128,992]{1,2,0:T(8,128)} %get-tuple-element.21), kind=kLoop, calls=%fused_computation.20 | loop fusion | flops 393216 | bytes 1572864 | tf_op jit(solution)/shard_map/add | solution.py:55
  39.8 0.0 copy-start.1
  39.8 0.0 copy-start.2
  39.8 1.3 %convert_reduce_fusion = f32[128,16,8]{0,2,1:T(8,128)S(1)} fusion(f32[1,128,16,2,8,4]{1,5,4,3,2,0:T(4,128)S(1)} %bitcast.265, f32[128,16,2]{0,2,1:T(2,128)S(1)} %bitcast.274, f32[1,128,16,2,8,4]{1,5,4,3,2,0:T(4,128)S(1)} %bitcast.263, f32[1,128,16,2,8,4]{1,5,4,3,2,0:T(4,128)S(1)} %bitcast.264, f32[128,16,2]{0,2,1:T(2,128)S(1)} %bitcast.273, ...), kind=kLoop, calls=%fused_computation.31 | loop fusion | flops 2867200 | bytes 3540992 | tf_op jit(solution)/shard_map/reduce_sum | solution.py:118
  41.1 0.1 reshape.897
  41.2 0.1 sine_multiply_fusion
  41.3 0.3 fusion.1
  41.6 0.6 copy.200
  42.2 3.3 %all-to-all-start = ((bf16[1,1,2,2,32,128]{5,3,2,1,0,4:T(2,128)(2,1)}), bf16[1,1,2,2,32,128]{5,3,2,1,0,4:T(2,128)(2,1)S(1)}, u32[]{:S(2)}, u32[]{:S(2)}) async-start(bf16[1,1,2,2,32,128]{5,3,2,1,0,4:T(2,128)(2,1)} %copy.200), calls=%async_computation | async-start | bytes 65536 | tf_op jit(solution)/shard_map/all_to_all | solution.py:164
  45.5 0.0 copy-done.1
  45.5 0.0 copy-done.2
  45.5 0.2 fusion.70
  45.7 0.7 multiply_reduce_fusion
  47.0 2.4 %all-to-all-done = bf16[1,1,2,2,32,128]{5,3,2,1,0,4:T(2,128)(2,1)S(1)} async-done(((bf16[1,1,2,2,32,128]{5,3,2,1,0,4:T(2,128)(2,1)}), bf16[1,1,2,2,32,128]{5,3,2,1,0,4:T(2,128)(2,1)S(1)}, u32[]{:S(2)}, u32[]{:S(2)}) %all-to-all-start) | async-done | bytes 32800 | tf_op jit(solution)/shard_map/all_to_all | solution.py:164
  49.5 3.7 %all_to_all.36 = bf16[1,1,4,2,16,128]{5,3,2,1,0,4:T(2,128)(2,1)S(1)} all-to-all(bf16[1,1,4,2,16,128]{5,3,2,1,0,4:T(2,128)(2,1)S(1)} %copy.203), channel_id=1, replica_groups=mesh['groups'=2,'tiles'=4,'freq'=2,'field'=2] {'field'}, dimensions={4} | all-to-all | bytes 65536 | tf_op jit(solution)/shard_map/all_to_all | solution.py:163
  53.2 13.4 %all-gather = bf16[2,4,1,4,2,8,128]{6,5,4,3,1,2,0:T(8,128)(2,1)S(1)} all-gather(bf16[2,1,1,4,2,8,128]{6,5,4,3,1,2,0:T(8,128)(2,1)S(1)} %bitcast.267), channel_id=2, replica_groups=mesh['groups'=2,'tiles'=4,'freq'=2,'field'=2] {'tiles'}, dimensions={1}, use_global_device_ids=true | all-gather | bytes 163840 | tf_op jit(solution)/shard_map/all_gather | solution.py:171
  66.7 0.6 gather_fusion.2
  67.3 0.5 fusion
  67.8 1.8 %copy.209 = f32[1,2,2,8,128,128]{5,4,3,2,1,0:T(8,128)} copy(f32[1,2,2,8,128,128]{4,5,2,1,3,0:T(8,128)S(1)} %fusion) | data formatting | bytes 4194304 | tf_op jit(solution)/shard_map/div | solution.py:144
  (43 shorter events, 0.6 us)
Async XLA Ops:
  3.3 1.1 %copy-start = (s32[4,4]{1,0:T(4,128)S(1)}, s32[4,4]{1,0:T(4,128)}, u32[]{:S(2)}) copy-start(s32[4,4]{1,0:T(4,128)} %param.8) | copy-start | bytes 196
  39.8 5.7 %copy-start.1 = (s32[4]{0:T(128)S(1)}, s32[4]{0:T(128)}, u32[]{:S(2)}) copy-start(s32[4]{0:T(128)} %param.6) | copy-start | bytes 52
  39.8 5.7 %copy-start.2 = (s32[1,2]{1,0:T(1,128)S(1)}, s32[1,2]{1,0:T(1,128)}, u32[]{:S(2)}) copy-start(s32[1,2]{1,0:T(1,128)} %param.9) | copy-start | bytes 28
  42.2 7.2 %all-to-all-start = ((bf16[1,1,2,2,32,128]{5,3,2,1,0,4:T(2,128)(2,1)}), bf16[1,1,2,2,32,128]{5,3,2,1,0,4:T(2,128)(2,1)S(1)}, u32[]{:S(2)}, u32[]{:S(2)}) async-start(bf16[1,1,2,2,32,128]{5,3,2,1,0,4:T(2,128)(2,1)} %copy.200), calls=%async_computation | async-start | bytes 65536 | tf_op jit(solution)/shard_map/all_to_all | solution.py:164
where the time goes:
time: 70 us; the launch traced here: 69.6 us
  blocking collectives  45.8 us (65%)
  local copies, waits for them, and re-layouts  9.18 us (13%)
  other arithmetic  7.23 us (10%)
  starting transfers between devices  3.26 us (5%)
  waiting for transfers between devices  2.42 us (3%)
  between operations  1.03 us (1%)
  matrix products  0.77 us (1%)
    all_gather x1, blocking collectives, shards(): lax.all_gather(tile_edges(field, SIDE), 'tiles', axis=0, tiled=True)  15.1 us
    all_gather x1, blocking collectives, shards(): lax.all_gather(inner_edges(field, SIDE), 'tiles', axis=0, tiled=True)  13.5 us
    all_gather x1, blocking collectives, shards(): every_band = lax.all_gather(banded, 'tiles', axis=1, tiled=True)  13.4 us
    all_to_all x1, blocking collectives, shards(): lax.all_to_all(lax.all_to_all(spectra[None], 'freq', split_axis=4, concat...  3.75 us
    all_to_all x1, starting transfers between devices, shards(): lax.all_to_all(spectra[None], 'freq', split_axis=4, concat_axis=2, tiled=...  3.26 us
    all_to_all x1, waiting for transfers between devices, shards(): lax.all_to_all(spectra[None], 'freq', split_axis=4, concat_axis=2, tiled=...  2.42 us
    convert_element_type x2, other arithmetic, smooth_step(): values = field.astype(jnp.float32)  2.21 us
    div x1, local copies, waits for them, and re-layouts, cross_density(): return cross / (partner.shape[2] * window_power)  1.81 us
  transfers between devices with their start and end apart: 1, of which 1 were waited for; matrix products, arithmetic and copies ran while one was open for 1% of the time, Pallas kernels for 0%

commit v1 on v0

--- a/solution.py
+++ b/solution.py
@@ -3,6 +3,7 @@
 import jax.numpy as jnp
 from jax import lax
 from jax.sharding import PartitionSpec as P
+from jax.lax import all_to_all, axis_size
 
 SIDE = 32
 SEGLEN = 64
@@ -160,12 +161,11 @@
     field = smooth_step(field, pick_rims(new_edges, near_local, code_local), SIDE)
     dft_table, window_power = window_table(SEGLEN)
     spectra = segment_spectra(coarse_sums(field, SIDE), dft_table)
+    search_kinds_on = lambda raw: jnp.concatenate(
+        all_to_all(jnp.stack(jnp.split(raw, axis_size("freq"), axis=4)), "freq", 0, 0), axis=2
+    )
     banded = lax.all_to_all(
-        lax.all_to_all(spectra[None], "freq", split_axis=4, concat_axis=2, tiled=True),
-        "field",
-        split_axis=4,
-        concat_axis=0,
-        tiled=True,
+        search_kinds_on(spectra[None]), "field", split_axis=4, concat_axis=0, tiled=True
     )
     partner_slots = slot_lookup(slot_tile_ids, paired_tile_ids)
     every_band = lax.all_gather(banded, "tiles", axis=1, tiled=True)

time: 70 us -> 70 us (level)
  no operation moved by 1% of the time
where the time goes in v1:
time: 70 us; the launch traced here: 69.6 us
  blocking collectives  45.8 us (65%)
  local copies, waits for them, and re-layouts  8.53 us (12%)
  other arithmetic  7.87 us (11%)
  starting transfers between devices  3.26 us (5%)
  waiting for transfers between devices  2.39 us (3%)
  between operations  1.03 us (1%)
  matrix products  0.77 us (1%)
    all_gather x1, blocking collectives, shards(): lax.all_gather(tile_edges(field, SIDE), 'tiles', axis=0, tiled=True)  15.1 us
    all_gather x1, blocking collectives, shards(): lax.all_gather(inner_edges(field, SIDE), 'tiles', axis=0, tiled=True)  13.5 us
    all_gather x1, blocking collectives, shards(): every_band = lax.all_gather(banded, 'tiles', axis=1, tiled=True)  13.4 us
    all_to_all x1, blocking collectives, shards(): lax.all_to_all(search_kinds_on(spectra[None]), 'field', split_axis=4, con...  3.75 us
    all_to_all x1, starting transfers between devices, shards(): all_to_all(jnp.stack(jnp.split(raw, axis_size('freq'), axis=4)), 'freq',...  3.26 us
    all_to_all x1, waiting for transfers between devices, shards(): all_to_all(jnp.stack(jnp.split(raw, axis_size('freq'), axis=4)), 'freq',...  2.39 us
    convert_element_type x2, other arithmetic, smooth_step(): values = field.astype(jnp.float32)  2.21 us
    div x1, local copies, waits for them, and re-layouts, cross_density(): return cross / (partner.shape[2] * window_power)  1.81 us
  transfers between devices with their start and end apart: 1, of which 1 were waited for; matrix products, arithmetic and copies ran while one was open for 1% of the time, Pallas kernels for 0%

profile of v1, /device:TPU:0, one launch (start us, length us, event | category | flops | bytes accessed | tf_op | source)
XLA Modules:
  0.0 69.6 jit_solution(3412914800968912235)
XLA Ops:
  0.1 0.8 %eq.65 = s32[16]{0:T(128)S(1)} reshape(s32[4,4]{1,0:T(4,128)} %param.7) | data formatting | bytes 128 | tf_op jit(solution)/shard_map/eq | solution.py:14
  0.9 0.7 %select_reduce_fusion = s32[16]{0:T(128)S(1)} fusion(s32[16]{0:T(128)S(1)} %eq.65, s32[4]{0:T(128)} %param.6), kind=kLoop, calls=%fused_computation.166 | loop fusion | flops 176 | bytes 144 | tf_op jit(solution)/shard_map/reduce_sum | solution.py:15
  1.6 0.1 reshape.899
  1.7 0.1 reshape.898
  1.8 0.1 broadcast_compare_fusion
  1.9 1.1 %copy.147 = bf16[1,1,128,1024]{2,3,1,0:T(8,128)(2,1)S(1)} copy(bf16[1,1,128,1024]{3,2,1,0:T(8,128)(2,1)} %param.5) | data formatting | bytes 524288 | tf_op args[0]
  3.0 0.1 slice.203
  3.0 0.1 slice.187
  3.1 0.1 slice.201
  3.2 0.1 slice.185
  3.3 0.0 copy-start
  3.3 1.0 %fusion.83 = (f32[1,128,992]{1,2,0:T(8,128)}, f32[1,128,992]{1,2,0:T(8,128)}) fusion(f32[1,128,1024]{1,2,0:T(8,128)S(1)} %bitcast_convert_fusion), kind=kLoop, calls=%fused_computation.200 | loop fusion | bytes 2031616 | tf_op jit(solution)/shard_map/slice | solution.py:49
  4.3 0.1 fusion.81
  4.4 0.0 copy-done
  4.5 0.1 reshape.905
  4.6 15.1 %all_gather.9 = bf16[4,4,128,32]{2,3,1,0:T(8,128)(2,1)S(1)} all-gather(bf16[1,4,128,32]{2,3,1,0:T(8,128)(2,1)S(1)} %pad_maximum_fusion.5), channel_id=1, replica_groups=mesh['groups'=2,'tiles'=4,'freq'=2,'field'=2] {'tiles'}, dimensions={0}, use_global_device_ids=true | all-gather | bytes 163840 | tf_op jit(solution)/shard_map/all_gather | solution.py:155
  19.7 0.6 gather_fusion
  20.3 0.1 rev.6
  20.3 0.1 fusion.77
  20.5 2.2 %fusion.14 = (f32[1,128,1024]{1,2,0:T(8,128)S(1)}, f32[1,128,1024]{1,2,0:T(8,128)S(1)}, f32[1,128,1024]{1,2,0:T(8,128)S(1)}, f32[1,128,1024]{1,2,0:T(8,128)S(1)}) fusion(f32[128,32]{0,1:T(8,128)S(1)} %get-tuple-element.45, f32[128,32]{0,1:T(8,128)S(1)} %get-tuple-element.44, pred[1024]{0:T(1024)(128)(4,1)S(1)} %get-tuple-element.77, ...), kind=kLoop, calls=%fused_computation.32 | loop fusion | flops 2097152 | bytes 4491264 | tf_op jit(solution)/shard_map/convert_element_type | solution.py:47
  22.7 1.0 %fusion.80 = (f32[1,128,992]{1,2,0:T(8,128)}, f32[1,128,992]{1,2,0:T(8,128)}) fusion(f32[1,128,1024]{1,2,0:T(8,128)S(1)} %get-tuple-element.9), kind=kLoop, calls=%fused_computation.197 | loop fusion | bytes 2031616 | tf_op jit(solution)/shard_map/slice | solution.py:50
  23.7 0.1 fusion.79
  23.8 13.5 %all_gather.10 = bf16[4,4,128,32]{2,3,1,0:T(8,128)(2,1)S(1)} all-gather(bf16[1,4,128,32]{2,3,1,0:T(8,128)(2,1)S(1)} %pad_maximum_fusion.6), channel_id=1, replica_groups=mesh['groups'=2,'tiles'=4,'freq'=2,'field'=2] {'tiles'}, dimensions={0}, use_global_device_ids=true | all-gather | bytes 163840 | tf_op jit(solution)/shard_map/all_gather | solution.py:156
  37.5 0.1 fusion.41
  37.6 0.1 fusion.33
  37.7 0.6 gather_fusion.1
  38.3 0.1 fusion.50
  38.5 1.2 %maximum_add_fusion.1 = f32[1,128,1024]{1,2,0:T(8,128)S(1)} fusion(f32[1,128,992]{1,2,0:T(8,128)} %get-tuple-element.22, f32[1,128,32]{1,2,0:T(8,128)S(1)} %get-tuple-element.52, f32[1,128,32]{1,2,0:T(8,128)S(1)} %get-tuple-element.51, f32[1,128,992]{1,2,0:T(8,128)} %get-tuple-element.21), kind=kLoop, calls=%fused_computation.20 | loop fusion | flops 393216 | bytes 1572864 | tf_op jit(solution)/shard_map/add | solution.py:56
  39.8 0.0 copy-start.1
  39.8 0.0 copy-start.2
  39.8 1.3 %convert_reduce_fusion = f32[128,16,8]{0,2,1:T(8,128)S(1)} fusion(f32[1,128,16,2,8,4]{1,5,4,3,2,0:T(4,128)S(1)} %bitcast.266, f32[128,16,2]{0,2,1:T(2,128)S(1)} %bitcast.274, f32[1,128,16,2,8,4]{1,5,4,3,2,0:T(4,128)S(1)} %bitcast.264, f32[1,128,16,2,8,4]{1,5,4,3,2,0:T(4,128)S(1)} %bitcast.265, f32[128,16,2]{0,2,1:T(2,128)S(1)} %bitcast.273, ...), kind=kLoop, calls=%fused_computation.31 | loop fusion | flops 2867200 | bytes 3540992 | tf_op jit(solution)/shard_map/reduce_sum | solution.py:119
  41.1 0.1 reshape.900
  41.2 0.1 sine_multiply_fusion
  41.3 0.3 fusion.1
  41.6 0.6 pad_maximum_fusion.7
  42.2 3.3 %all-to-all-start = ((bf16[2,1,1,2,2,16,128]{6,5,4,3,2,1,0:T(8,128)(2,1)}), bf16[2,1,1,2,2,16,128]{6,5,4,3,2,1,0:T(8,128)(2,1)S(1)}, u32[]{:S(2)}, u32[]{:S(2)}) async-start(bf16[2,1,1,2,2,16,128]{6,5,4,3,2,1,0:T(8,128)(2,1)} %pad_maximum_fusion.7), calls=%async_computation | async-start | bytes 65536 | tf_op jit(solution)/shard_map/all_to_all | solution.py:165
  45.5 0.0 copy-done.1
  45.5 0.0 copy-done.2
  45.5 0.2 fusion.70
  45.7 0.7 multiply_reduce_fusion
  47.0 2.4 %all-to-all-done = bf16[2,1,1,2,2,16,128]{6,5,4,3,2,1,0:T(8,128)(2,1)S(1)} async-done(((bf16[2,1,1,2,2,16,128]{6,5,4,3,2,1,0:T(8,128)(2,1)}), bf16[2,1,1,2,2,16,128]{6,5,4,3,2,1,0:T(8,128)(2,1)S(1)}, u32[]{:S(2)}, u32[]{:S(2)}) %all-to-all-start) | async-done | bytes 32800 | tf_op jit(solution)/shard_map/all_to_all | solution.py:165
  49.5 3.7 %all_to_all.23 = bf16[1,1,4,2,16,128]{5,3,2,1,0,4:T(2,128)(2,1)S(1)} all-to-all(bf16[1,1,4,2,16,128]{5,3,2,1,0,4:T(2,128)(2,1)S(1)} %copy.166), channel_id=1, replica_groups=mesh['groups'=2,'tiles'=4,'freq'=2,'field'=2] {'field'}, dimensions={4} | all-to-all | bytes 65536 | tf_op jit(solution)/shard_map/all_to_all | solution.py:167
  53.2 13.4 %all-gather = bf16[2,4,1,4,2,8,128]{6,5,4,3,1,2,0:T(8,128)(2,1)S(1)} all-gather(bf16[2,1,1,4,2,8,128]{6,5,4,3,1,2,0:T(8,128)(2,1)S(1)} %bitcast.268), channel_id=2, replica_groups=mesh['groups'=2,'tiles'=4,'freq'=2,'field'=2] {'tiles'}, dimensions={1}, use_global_device_ids=true | all-gather | bytes 163840 | tf_op jit(solution)/shard_map/all_gather | solution.py:171
  66.7 0.6 gather_fusion.2
  67.3 0.5 fusion
  67.8 1.8 %copy.172 = f32[1,2,2,8,128,128]{5,4,3,2,1,0:T(8,128)} copy(f32[1,2,2,8,128,128]{4,5,2,1,3,0:T(8,128)S(1)} %fusion) | data formatting | bytes 4194304 | tf_op jit(solution)/shard_map/div | solution.py:145
  (42 shorter events, 0.6 us)
Async XLA Ops:
  3.3 1.1 %copy-start = (s32[4,4]{1,0:T(4,128)S(1)}, s32[4,4]{1,0:T(4,128)}, u32[]{:S(2)}) copy-start(s32[4,4]{1,0:T(4,128)} %param.8) | copy-start | bytes 196
  39.8 5.7 %copy-start.1 = (s32[4]{0:T(128)S(1)}, s32[4]{0:T(128)}, u32[]{:S(2)}) copy-start(s32[4]{0:T(128)} %param.6) | copy-start | bytes 52
  39.8 5.7 %copy-start.2 = (s32[1,2]{1,0:T(1,128)S(1)}, s32[1,2]{1,0:T(1,128)}, u32[]{:S(2)}) copy-start(s32[1,2]{1,0:T(1,128)} %param.9) | copy-start | bytes 28
  42.2 7.2 %all-to-all-start = ((bf16[2,1,1,2,2,16,128]{6,5,4,3,2,1,0:T(8,128)(2,1)}), bf16[2,1,1,2,2,16,128]{6,5,4,3,2,1,0:T(8,128)(2,1)S(1)}, u32[]{:S(2)}, u32[]{:S(2)}) async-start(bf16[2,1,1,2,2,16,128]{6,5,4,3,2,1,0:T(8,128)(2,1)} %pad_maximum_fusion.7), calls=%async_computation | async-start | bytes 65536 | tf_op jit(solution)/shard_map/all_to_all | solution.py:165
